TPU v7x, 128 devices: a whole 4x4x4 slice. The times are simulated.
128 devices in a mesh: req: 32 (over y, x, core), mlp: 4 (over z).
Axes of the slice: x: 4, y: 4, z: 4, core: 2. Of those that a mesh axis runs over, the one named last changes fastest.
Arguments:
- states: bfloat16 [8192, 2560], P('req')
- attn_gain: float32 [2560], replicated, may hold values from 0.1 to 1.9
- query_matrix: bfloat16 [2560, 2048], P(None, 'mlp')
- key_matrix: bfloat16 [2560, 1024], P(None, 'mlp')
- value_matrix: bfloat16 [2560, 1024], P(None, 'mlp'), may hold values from -0.125 to 0.125
- query_gain: float32 [256], replicated
- key_gain: float32 [256], replicated
- out_weight: bfloat16 [2048, 2560], P('mlp'), may hold values from -0.125 to 0.125
- post_gain: float32 [2560], replicated, may hold values from 0.1 to 1.9
- ffw_gain: float32 [2560], replicated, may hold values from 0.1 to 1.9
- gate_weight: bfloat16 [2560, 10240], P(None, 'req'), may hold values from -0.125 to 0.125
- up_weight: bfloat16 [2560, 10240], P(None, 'req'), may hold values from -0.125 to 0.125
- down_weight: bfloat16 [10240, 2560], P('req'), may hold values from -0.0625 to 0.0625
- post_ffw_gain: float32 [2560], replicated, may hold values from 0.1 to 1.9
- prefix_key_cache: bfloat16 [32, 512, 1024], P('req', None, 'mlp')
- prefix_value_cache: bfloat16 [32, 512, 1024], P('req', None, 'mlp'), may hold values from -6 to 6
- segment: int32 [8192], P('req'), may hold values from 0 to 15, as said below
- prefix_id: int32 [8192], P('req'), may hold values from 0 to 31, as said below
- owner_map: int32 [32], replicated, may hold values from 0 to 31, each once
Outputs:
- layer_out: bfloat16 [8192, 2560], P(('req', 'mlp'))
Inputs may be any that keep to these rules, and one draw needn't show every extreme that they name: Within each block of 256 rows, equal segment values mark one request and occupy contiguous rows; requests hold 16 or 32 tokens. `prefix_id`: all tokens of one request name the same prefix group. In each block of 256 rows at most 32 rows name prefix groups of the same owner, and one prefix group is named by exactly 32 rows of every block.
All inputs are finite; a program needn't handle non-finite values.
Results may differ from a plain program's by a relative error of at most 0.017.
The roundings to bfloat16 on the way count: a program that leaves them out, or rounds other values in their place, can miss the bound.
Values may be sent and summed in bfloat16 or wider, within the bound.
A program may use at most 128 MiB of HBM per device.

v0:
```python
import jax
import jax.numpy as jnp
from jax import lax
from jax.sharding import PartitionSpec as P

CAP = 32
EPS = 1e-06


def normed(values_in, gain_vec):
    return (
        values_in
        * lax.rsqrt(jnp.mean(values_in * values_in, axis=-1, keepdims=True) + EPS)
        * gain_vec
    )


def local_attention(query_rows, key_rows, value_rows, segment_rows, score_scale):
    scores = (
        jnp.einsum("tgqd,sgd->gqts", query_rows, key_rows, preferred_element_type=jnp.float32)
        * score_scale
    )
    row_count = segment_rows.shape[0]
    token_position = jnp.arange(row_count, dtype=jnp.int32)
    allowed = (segment_rows[:, None] == segment_rows[None, :]) & (
        token_position[:, None] >= token_position[None, :]
    )
    scores = jnp.where(allowed, scores, -jnp.inf)
    row_max = jnp.max(scores, axis=-1, keepdims=True)
    powers = jnp.exp(scores - row_max)
    row_sum = jnp.sum(powers, axis=-1, keepdims=True)
    weights = (powers / row_sum).astype(jnp.bfloat16)
    mixed = jnp.einsum("gqts,sgd->tgqd", weights, value_rows, preferred_element_type=jnp.float32)
    log_total = jnp.transpose((row_max + jnp.log(row_sum))[..., 0], (2, 0, 1))
    return (mixed, log_total)


def prefix_partials(incoming, stored_keys, stored_values, score_scale):
    sources, slot_count, head_cols = incoming.shape
    kv_heads = stored_keys.shape[1]
    head_dim = stored_keys.shape[2]
    query_group_width = head_cols // (kv_heads * head_dim)
    query_rows = incoming.reshape(sources * slot_count, kv_heads, query_group_width, head_dim)
    scores = (
        jnp.einsum("rgqd,kgd->rgqk", query_rows, stored_keys, preferred_element_type=jnp.float32)
        * score_scale
    )
    row_max = jnp.max(scores, axis=-1, keepdims=True)
    powers = jnp.exp(scores - row_max)
    row_sum = jnp.sum(powers, axis=-1, keepdims=True)
    weights = (powers / row_sum).astype(jnp.bfloat16)
    mixed = jnp.einsum("rgqk,kgd->rgqd", weights, stored_values, preferred_element_type=jnp.float32)
    mixed = lax.optimization_barrier(mixed.astype(jnp.bfloat16)).astype(jnp.float32)
    log_total = row_max[..., 0] + jnp.log(row_sum[..., 0])
    return (
        mixed.reshape(sources, slot_count, head_cols),
        log_total.reshape(sources, slot_count, kv_heads * query_group_width),
    )


def body(
    states,
    attn_gain,
    query_matrix,
    key_matrix,
    value_matrix,
    query_gain,
    key_gain,
    out_weight,
    post_gain,
    ffw_gain,
    gate_weight,
    up_weight,
    down_weight,
    post_ffw_gain,
    prefix_key_cache,
    prefix_value_cache,
    segment,
    prefix_id,
    owner_map,
):
    row_count = states.shape[0]
    head_dim = query_gain.shape[0]
    kv_heads = key_matrix.shape[1] // head_dim
    head_cols = query_matrix.shape[1]
    query_group_width = head_cols // (kv_heads * head_dim)
    score_scale = head_dim ** (-0.5)
    req_count = lax.axis_size("req")
    mlp_count = lax.axis_size("mlp")
    mlp_index = lax.axis_index("mlp")
    quarter = row_count // mlp_count
    states_f = states.astype(jnp.float32)
    normalized_input = normed(states_f, attn_gain).astype(jnp.bfloat16)
    unnormed_queries = jnp.dot(
        normalized_input, query_matrix, preferred_element_type=jnp.float32
    ).reshape(row_count, kv_heads, query_group_width, head_dim)
    query_vectors = normed(unnormed_queries, query_gain).astype(jnp.bfloat16)
    unnormed_keys = jnp.dot(
        normalized_input, key_matrix, preferred_element_type=jnp.float32
    ).reshape(row_count, kv_heads, head_dim)
    key_vectors = normed(unnormed_keys, key_gain).astype(jnp.bfloat16)
    value_vectors = (
        jnp.dot(normalized_input, value_matrix, preferred_element_type=jnp.float32)
        .astype(jnp.bfloat16)
        .reshape(row_count, kv_heads, head_dim)
    )
    prefix_count = owner_map.shape[0]
    prefix_onehot = (
        prefix_id[:, None] == jnp.arange(prefix_count, dtype=jnp.int32)[None, :]
    ).astype(jnp.int32)
    target = jnp.sum(prefix_onehot * owner_map[None, :], axis=1)
    to_owner = (target[:, None] == jnp.arange(req_count, dtype=jnp.int32)[None, :]).astype(
        jnp.float32
    )
    token_position = jnp.arange(row_count, dtype=jnp.int32)
    earlier = (token_position[:, None] > token_position[None, :]).astype(jnp.float32)
    counts = jnp.dot(earlier, to_owner, precision=lax.Precision.HIGHEST)
    slot_index = jnp.sum(to_owner * counts, axis=1).astype(jnp.int32)
    place_row = target * CAP + slot_index
    placing = (place_row[None, :] == jnp.arange(req_count * CAP, dtype=jnp.int32)[:, None]).astype(
        jnp.bfloat16
    )
    outgoing = (
        jnp.dot(
            placing, query_vectors.reshape(row_count, head_cols), preferred_element_type=jnp.float32
        )
        .astype(jnp.bfloat16)
        .reshape(req_count, CAP, head_cols)
    )
    stored_keys = prefix_key_cache[0].reshape(-1, kv_heads, head_dim)
    stored_values = prefix_value_cache[0].reshape(-1, kv_heads, head_dim)
    suffix_output, suffix_log_sum = local_attention(
        query_vectors, key_vectors, value_vectors, segment, score_scale
    )
    mixed, log_total = prefix_partials(
        lax.all_to_all(outgoing, "req", split_axis=0, concat_axis=0, tiled=True),
        stored_keys,
        stored_values,
        score_scale,
    )
    back_out = lax.all_to_all(
        mixed.astype(jnp.bfloat16), "req", split_axis=0, concat_axis=0, tiled=True
    ).astype(mixed.dtype)
    back_lse = lax.all_to_all(
        log_total.astype(jnp.bfloat16), "req", split_axis=0, concat_axis=0, tiled=True
    ).astype(log_total.dtype)
    prefix_out = back_out.reshape(req_count * CAP, head_cols)[place_row].reshape(
        row_count, kv_heads, query_group_width, head_dim
    )
    prefix_lse = back_lse.reshape(req_count * CAP, kv_heads * query_group_width)[place_row].reshape(
        row_count, kv_heads, query_group_width
    )
    prefix_out, prefix_lse = (prefix_out, prefix_lse)
    blend = jax.nn.sigmoid(prefix_lse - suffix_log_sum)[..., None]
    attended = (
        (blend * prefix_out + (1.0 - blend) * suffix_output)
        .astype(jnp.bfloat16)
        .reshape(row_count, head_cols)
    )
    partial_value = jnp.dot(attended, out_weight, preferred_element_type=jnp.float32)
    full_sum = lax.psum(partial_value.astype(jnp.bfloat16), "mlp").astype(jnp.float32)
    summed = lax.dynamic_slice_in_dim(full_sum, mlp_index * quarter, quarter, 0)
    own_rows = lax.dynamic_slice_in_dim(states_f, mlp_index * quarter, quarter, 0)
    residual = own_rows + normed(summed, post_gain)
    ffw_in = normed(residual, ffw_gain).astype(jnp.bfloat16)
    piece = lax.all_gather(ffw_in, "req", axis=0, tiled=True)
    gate_proj = jnp.dot(piece, gate_weight, preferred_element_type=jnp.float32)
    up_proj = jnp.dot(piece, up_weight, preferred_element_type=jnp.float32)
    hidden = (jax.nn.gelu(gate_proj, approximate=True) * up_proj).astype(jnp.bfloat16)
    down_sum = lax.psum_scatter(
        jnp.dot(hidden, down_weight, preferred_element_type=jnp.float32).astype(jnp.bfloat16),
        "req",
        scatter_dimension=0,
        tiled=True,
    ).astype(jnp.float32)
    return (residual + normed(down_sum, post_ffw_gain)).astype(jnp.bfloat16)


def solution(mesh):
    return jax.shard_map(
        body,
        mesh=mesh,
        in_specs=(
            P("req", None),
            P(),
            P(None, "mlp"),
            P(None, "mlp"),
            P(None, "mlp"),
            P(),
            P(),
            P("mlp", None),
            P(),
            P(),
            P(None, "req"),
            P(None, "req"),
            P("req", None),
            P(),
            P("req", None, "mlp"),
            P("req", None, "mlp"),
            P("req"),
            P("req"),
            P(),
        ),
        out_specs=P(("req", "mlp"), None),
        check_vma=False,
    )
```

profile of v0, /device:TPU:0, one launch (start us, length us, event | category | flops | bytes accessed | tf_op | source)
XLA Modules:
  0.0 342.5 jit_solution(14212697419758735946)
XLA Ops:
  6.5 0.9 select_reduce_fusion
  7.5 0.2 fusion.29
  7.7 1.7 multiply_reduce_fusion
  9.4 0.7 broadcast_bitcast_fusion
  10.0 4.1 %fusion.66 = (f32[256,512]{1,0:T(8,128)}, f32[256,512]{1,0:T(8,128)}) fusion(bf16[2560,512]{1,0:T(8,128)(2,1)} %param.21, f32[2560]{0:T(1024)} %param.20, f32[256]{0:T(256)S(1)} %add_rsqrt_fusion.2, bf16[256,2560]{1,0:T(8,128)(2,1)} %param.19), kind=kOutput, calls=%fused_computation.108 | convolution fusion | flops 673841152 | bytes 4992000 | tf_op jit(solution)/shard_map/dot_general | solution.py:94
  14.1 1.4 mul.266
  15.5 0.3 reduce_sum.93
  15.9 0.3 mul.267
  16.3 1.2 multiply_convert_fusion.2
  17.4 1.5 convolution_convert_fusion.2
  18.9 7.5 %all-to-all-start = ((bf16[32,32,512]{2,1,0:T(8,128)(2,1)}), bf16[32,32,512]{2,1,0:T(8,128)(2,1)}, u32[]{:S(2)}, u32[]{:S(2)}) async-start(bf16[32,32,512]{2,1,0:T(8,128)(2,1)} %bitcast.130), calls=%async_computation | async-start | bytes 2097152 | tf_op jit(solution)/shard_map/all_to_all | solution.py:136
  26.5 0.1 fusion.47
  26.6 3.2 multiply_reduce_fusion.2
  29.8 13.9 %all-to-all-done = bf16[32,32,512]{2,1,0:T(8,128)(2,1)} async-done(((bf16[32,32,512]{2,1,0:T(8,128)(2,1)}), bf16[32,32,512]{2,1,0:T(8,128)(2,1)}, u32[]{:S(2)}, u32[]{:S(2)}) %all-to-all-start) | async-done | bytes 1048608 | tf_op jit(solution)/shard_map/all_to_all | solution.py:136
  43.8 2.2 reshape.279
  46.0 2.0 bitcast_reduce_fusion
  48.0 1.9 copy-done.1
  49.9 0.7 fusion.1
  50.6 0.1 convert_element_type.106
  50.7 0.6 copy.99
  51.3 3.8 %all-to-all-start.1 = ((bf16[32,32,2]{1,2,0:T(2,128)(2,1)}), bf16[32,32,2]{1,2,0:T(2,128)(2,1)S(1)}, u32[]{:S(2)}, u32[]{:S(2)}) async-start(bf16[32,32,2]{1,2,0:T(2,128)(2,1)} %copy.99), calls=%async_computation.1 | async-start | bytes 32768 | tf_op jit(solution)/shard_map/all_to_all | solution.py:144
  55.1 3.5 %fusion.16 = bf16[1024,1,2,256]{3,0,2,1:T(8,128)(2,1)S(1)} fusion(f32[1024,2]{0,1:T(2,128)S(1)} %fusion.1, f32[1024,2]{0,1:T(2,128)S(1)} %get-tuple-element.9, f32[1024,2,512]{0,2,1:T(8,128)} %copy-done.1, bf16[1,512,256]{2,1,0:T(8,128)(2,1)S(1)} %copy-done.8), kind=kOutput, calls=%fused_computation.26 | convolution fusion | flops 541589504 | bytes 5521408 | tf_op jit(solution)/shard_map/rgqk,kgd->rgqd/dot_general | solution.py:52
  58.6 2.1 copy.106
  60.7 2.6 convert_element_type.114
  63.3 7.5 %all-to-all-start.2 = ((bf16[32,32,512]{2,1,0:T(8,128)(2,1)}), bf16[32,32,512]{2,1,0:T(8,128)(2,1)}, u32[]{:S(2)}, u32[]{:S(2)}) async-start(bf16[32,32,512]{2,1,0:T(8,128)(2,1)} %convert_element_type.114), calls=%async_computation.2 | async-start | bytes 2097152 | tf_op jit(solution)/shard_map/all_to_all | solution.py:141
  70.8 0.2 all-reduce.2.cloned.1.call-start
  71.1 0.4 fusion.67
  71.5 0.1 fusion.40
  71.6 0.7 copy-done.2
  72.2 0.3 copy.114
  72.5 0.7 gather_fusion
  73.4 14.8 %all-to-all-done.2 = bf16[32,32,512]{2,1,0:T(8,128)(2,1)} async-done(((bf16[32,32,512]{2,1,0:T(8,128)(2,1)}), bf16[32,32,512]{2,1,0:T(8,128)(2,1)}, u32[]{:S(2)}, u32[]{:S(2)}) %all-to-all-start.2) | async-done | bytes 1048608 | tf_op jit(solution)/shard_map/all_to_all | solution.py:141
  88.1 2.9 bitcast_convert_fusion
  91.0 2.8 gather_fusion.1
  93.8 1.0 copy.107
  94.8 2.9 fusion.26
  97.7 1.9 convolution_convert_fusion.1
  99.7 3.2 convert_element_type.100
  102.9 43.6 %all-reduce.2.cloned.1.call-done = bf16[256,2560]{1,0:T(8,128)(2,1)} async-done(((bf16[256,2560]{1,0:T(8,128)(2,1)}), bf16[256,2560]{1,0:T(8,128)(2,1)}) %all-reduce.2.cloned.1.call-update) | async-done | bytes 1310736 | tf_op jit(solution)/shard_map/psum | solution.py:161
  146.5 1.1 fusion.34
  147.7 1.5 multiply_reduce_fusion.1
  149.2 2.1 multiply_convert_fusion.1
  151.4 58.3 %all-gather.2.cloned.1.call-done = bf16[2048,2560]{1,0:T(8,128)(2,1)} async-done(((bf16[64,2560]{1,0:T(8,128)(2,1)}), bf16[2048,2560]{1,0:T(8,128)(2,1)}) %all-gather.2.cloned.1.call-update) | async-done | bytes 10485776 | tf_op jit(solution)/shard_map/all_gather | solution.py:166
  209.7 9.5 %fusion.68 = f32[2048,320]{0,1:T(8,128)} fusion(bf16[2048,2560]{1,0:T(8,128)(2,1)} %all-gather.2.cloned.1.call-done, bf16[2560,320]{0,1:T(8,128)(2,1)} %param.29), kind=kOutput, calls=%fused_computation.110 | convolution fusion | flops 3355443200 | bytes 14745600 | tf_op jit(solution)/shard_map/dot_general | solution.py:167
  219.2 15.6 %convolution_convert_fusion = bf16[2048,2560]{1,0:T(8,128)(2,1)} fusion(bf16[320,2560]{1,0:T(8,128)(2,1)} %param.31, bf16[2048,2560]{1,0:T(8,128)(2,1)} %all-gather.2.cloned.1.call-done, bf16[2560,320]{0,1:T(8,128)(2,1)} %param.30, f32[2048,320]{0,1:T(8,128)} %fusion.68), kind=kOutput, calls=%fused_computation.2 | convolution fusion | flops 6722682880 | bytes 26869760 | tf_op jit(solution)/shard_map/dot_general | solution.py:171
  234.9 97.7 %reduce-scatter.2.cloned.1.call-done = bf16[64,2560]{1,0:T(8,128)(2,1)} async-done(((bf16[2048,2560]{1,0:T(8,128)(2,1)}), bf16[64,2560]{1,0:T(8,128)(2,1)}) %reduce-scatter.2.cloned.1.call-update) | async-done | bytes 327696 | tf_op jit(solution)/shard_map/reduce_scatter | solution.py:170
  332.5 1.1 fusion.35
  333.7 2.3 fusion.38
  (45 shorter events, 0.4 us)
Async XLA Ops:
  6.5 91.2 %copy-start = (bf16[512,2560]{1,0:T(8,128)(2,1)S(1)}, bf16[512,2560]{1,0:T(8,128)(2,1)}, u32[]{:S(2)}) copy-start(bf16[512,2560]{1,0:T(8,128)(2,1)} %param.26) | copy-start | bytes 7864324
  16.2 10.2 %copy-start.7 = (s32[256]{0:T(256)S(1)}, s32[256]{0:T(256)}, u32[]{:S(2)}) copy-start(s32[256]{0:T(256)} %param.35) | copy-start | bytes 3076
  16.3 10.3 %copy-start.9 = (f32[2560]{0:T(1024)S(1)}, f32[2560]{0:T(1024)}, u32[]{:S(2)}) copy-start(f32[2560]{0:T(1024)} %param.20) | copy-start | bytes 30724
  18.9 24.9 %all-to-all-start = ((bf16[32,32,512]{2,1,0:T(8,128)(2,1)}), bf16[32,32,512]{2,1,0:T(8,128)(2,1)}, u32[]{:S(2)}, u32[]{:S(2)}) async-start(bf16[32,32,512]{2,1,0:T(8,128)(2,1)} %bitcast.130), calls=%async_computation | async-start | bytes 2097152 | tf_op jit(solution)/shard_map/all_to_all | solution.py:136
  26.6 19.4 %copy-start.3 = (bf16[1,512,256]{2,1,0:T(8,128)(2,1)S(1)}, bf16[1,512,256]{2,1,0:T(8,128)(2,1)}, u32[]{:S(2)}) copy-start(bf16[1,512,256]{2,1,0:T(8,128)(2,1)} %param.33) | copy-start | bytes 786436
  48.0 1.9 copy-start.1
  48.0 7.1 %copy-start.8 = (bf16[1,512,256]{2,1,0:T(8,128)(2,1)S(1)}, bf16[1,512,256]{2,1,0:T(8,128)(2,1)}, u32[]{:S(2)}) copy-start(bf16[1,512,256]{2,1,0:T(8,128)(2,1)} %param.34) | copy-start | bytes 786436
  51.3 12.0 %all-to-all-start.1 = ((bf16[32,32,2]{1,2,0:T(2,128)(2,1)}), bf16[32,32,2]{1,2,0:T(2,128)(2,1)S(1)}, u32[]{:S(2)}, u32[]{:S(2)}) async-start(bf16[32,32,2]{1,2,0:T(2,128)(2,1)} %copy.99), calls=%async_computation.1 | async-start | bytes 32768 | tf_op jit(solution)/shard_map/all_to_all | solution.py:144
  60.7 10.3 %copy-start.11 = (f32[256]{0:T(256)S(1)}, f32[256]{0:T(256)}, u32[]{:S(2)}) copy-start(f32[256]{0:T(256)} %param.25) | copy-start | bytes 3076
  60.7 10.3 %copy-start.12 = (f32[256,256]{0,1:T(8,128)S(1)}, f32[256,256]{0,1:T(8,128)}, u32[]{:S(2)}) copy-start(f32[256,256]{0,1:T(8,128)} %get-tuple-element.12) | copy-start | bytes 786436
  63.3 24.8 %all-to-all-start.2 = ((bf16[32,32,512]{2,1,0:T(8,128)(2,1)}), bf16[32,32,512]{2,1,0:T(8,128)(2,1)}, u32[]{:S(2)}, u32[]{:S(2)}) async-start(bf16[32,32,512]{2,1,0:T(8,128)(2,1)} %convert_element_type.114), calls=%async_computation.2 | async-start | bytes 2097152 | tf_op jit(solution)/shard_map/all_to_all | solution.py:141
  70.8 75.7 %all-reduce.2.cloned.1.call-start = ((), (), s32[]{:S(2)}) async-start(), calls=%async_computation.4 | async-start | bytes 2621440 | tf_op jit(solution)/shard_map/psum | solution.py:161
  71.4 0.8 copy-start.2
  91.0 3.8 %copy-start.10 = (f32[2560]{0:T(1024)S(1)}, f32[2560]{0:T(1024)}, u32[]{:S(2)}) copy-start(f32[2560]{0:T(1024)} %param.20) | copy-start | bytes 30724
  99.6 48.0 %copy-start.4 = (f32[2560]{0:T(1024)S(1)}, f32[2560]{0:T(1024)}, u32[]{:S(2)}) copy-start(f32[2560]{0:T(1024)} %param.27) | copy-start | bytes 30724
  99.7 110.0 %all-gather.2.cloned.1.call-start = ((), (), s32[]{:S(2)}) async-start(), calls=%async_computation.5 | async-start | bytes 10813440 | tf_op jit(solution)/shard_map/all_gather | solution.py:166
  99.7 49.4 %copy-start.5 = (f32[2560]{0:T(1024)S(1)}, f32[2560]{0:T(1024)}, u32[]{:S(2)}) copy-start(f32[2560]{0:T(1024)} %param.28) | copy-start | bytes 30724
  151.3 181.2 %reduce-scatter.2.cloned.1.call-start = ((), (), s32[]{:S(2)}) async-start(), calls=%async_computation.6 | async-start | bytes 10813440 | tf_op jit(solution)/shard_map/reduce_scatter | solution.py:170
  234.8 98.9 %copy-start.6 = (f32[2560]{0:T(1024)S(1)}, f32[2560]{0:T(1024)}, u32[]{:S(2)}) copy-start(f32[2560]{0:T(1024)} %param.32) | copy-start | bytes 30724
Sparse Core Ops, SparseCore 0:
  99.8 46.6 all-reduce.1
  151.5 58.1 all-gather.1
  235.0 97.5 reduce-scatter.1
where the time goes:
time: 343 us
  waiting for transfers between devices  228 us (66%)
  matrix products  44.8 us (13%)
  other arithmetic  19.4 us (6%)
  starting transfers between devices  19.1 us (6%)
  local copies, waits for them, and re-layouts  17.5 us (5%)
  between operations  13.4 us (4%)
    reduce_scatter x1, waiting for transfers between devices, body(): lax.psum_scatter(jnp.dot(hidden, down_weight, preferred_element_type=jnp....  97.7 us
    all_gather x1, waiting for transfers between devices, body(): piece = lax.all_gather(ffw_in, 'req', axis=0, tiled=True)  58.3 us
    psum x1, waiting for transfers between devices, body(): lax.psum(partial_value.astype(jnp.bfloat16), 'mlp').astype(jnp.float32)  43.6 us
    dot_general x1, matrix products, body(): jnp.dot(hidden, down_weight, preferred_element_type=jnp.float32)  15.6 us
    all_to_all x1, waiting for transfers between devices, body(): lax.all_to_all(mixed.astype(jnp.bfloat16), 'req', split_axis=0, concat_ax...  14.8 us
    all_to_all x1, waiting for transfers between devices, body(): lax.all_to_all(outgoing, 'req', split_axis=0, concat_axis=0, tiled=True)  13.9 us
    dot_general x1, matrix products, body(): gate_proj = jnp.dot(piece, gate_weight, preferred_element_type=jnp.float32)  9.52 us
    all_to_all x1, starting transfers between devices, body(): lax.all_to_all(outgoing, 'req', split_axis=0, concat_axis=0, tiled=True)  7.53 us
  transfers between devices with their start and end apart: 6, of which 5 were waited for; matrix products, arithmetic and copies ran while one was open for 5% of the time, Pallas kernels for 0%

commit v1 on v0

--- a/solution.py
+++ b/solution.py
@@ -163,7 +163,10 @@
     own_rows = lax.dynamic_slice_in_dim(states_f, mlp_index * quarter, quarter, 0)
     residual = own_rows + normed(summed, post_gain)
     ffw_in = normed(residual, ffw_gain).astype(jnp.bfloat16)
-    piece = lax.all_gather(ffw_in, "req", axis=0, tiled=True)
+    count = lax.axis_size("req")
+    blocks = jnp.stack([ffw_in for _ in range(count)])
+    blocks = lax.all_to_all(blocks, "req", split_axis=0, concat_axis=0)
+    piece = jnp.concatenate(blocks, axis=0)
     gate_proj = jnp.dot(piece, gate_weight, preferred_element_type=jnp.float32)
     up_proj = jnp.dot(piece, up_weight, preferred_element_type=jnp.float32)
     hidden = (jax.nn.gelu(gate_proj, approximate=True) * up_proj).astype(jnp.bfloat16)

time: 343 us -> 411 us (1.20)
  blocking collectives: 0 us -> 126 us
  waiting for transfers between devices: 228 us -> 169 us
    all_to_all x0 -> x1, blocking collectives: none -> 126 us  [body(): blocks = lax.all_to_all(blocks, 'req', split_axis=0, concat_axis=0)]
    all_gather x1 -> x0, waiting for transfers between devices: 58.3 us -> none  [body(): piece = lax.all_gather(ffw_in, 'req', axis=0, tiled=True)]
  transfers between devices with their start and end apart: 6 -> 5, of which waited for: 5 -> 4; matrix products, arithmetic and copies ran while one was open for 5% -> 4% of each run, Pallas kernels for 0% -> 0%
where the time goes in v1:
time: 411 us; the launch traced here: 410 us
  waiting for transfers between devices  169 us (41%)
  blocking collectives  126 us (31%)
  matrix products  45 us (11%)
  other arithmetic  20.9 us (5%)
  starting transfers between devices  19.1 us (5%)
  local copies, waits for them, and re-layouts  16.8 us (4%)
  between operations  13.7 us (3%)
    all_to_all x1, blocking collectives, body(): blocks = lax.all_to_all(blocks, 'req', split_axis=0, concat_axis=0)  126 us
    reduce_scatter x1, waiting for transfers between devices, body(): lax.psum_scatter(jnp.dot(hidden, down_weight, preferred_element_type=jnp....  96.8 us
    psum x1, waiting for transfers between devices, body(): lax.psum(partial_value.astype(jnp.bfloat16), 'mlp').astype(jnp.float32)  43.6 us
    dot_general x1, matrix products, body(): jnp.dot(hidden, down_weight, preferred_element_type=jnp.float32)  15.6 us
    all_to_all x1, waiting for transfers between devices, body(): lax.all_to_all(mixed.astype(jnp.bfloat16), 'req', split_axis=0, concat_ax...  14.8 us
    all_to_all x1, waiting for transfers between devices, body(): lax.all_to_all(outgoing, 'req', split_axis=0, concat_axis=0, tiled=True)  13.9 us
  transfers between devices with their start and end apart: 5, of which 4 were waited for; matrix products, arithmetic and copies ran while one was open for 4% of the time, Pallas kernels for 0%

profile of v1, /device:TPU:0, one launch (start us, length us, event | category | flops | bytes accessed | tf_op | source)
XLA Modules:
  0.0 410.2 jit_solution(17970818340888499431)
XLA Ops:
  6.5 0.9 select_reduce_fusion
  7.5 0.2 fusion.29
  7.7 1.7 multiply_reduce_fusion
  9.4 0.7 broadcast_bitcast_fusion
  10.0 4.1 fusion.66
  14.1 1.4 mul.266
  15.5 0.3 reduce_sum.93
  15.9 0.3 mul.267
  16.3 1.2 multiply_convert_fusion.2
  17.4 1.5 convolution_convert_fusion.2
  18.9 7.5 %all-to-all-start = ((bf16[32,32,512]{2,1,0:T(8,128)(2,1)}), bf16[32,32,512]{2,1,0:T(8,128)(2,1)}, u32[]{:S(2)}, u32[]{:S(2)}) async-start(bf16[32,32,512]{2,1,0:T(8,128)(2,1)} %bitcast.131), calls=%async_computation | async-start | bytes 2097152 | tf_op jit(solution)/shard_map/all_to_all | solution.py:136
  26.5 0.1 fusion.47
  26.6 3.2 multiply_reduce_fusion.2
  29.8 13.9 %all-to-all-done = bf16[32,32,512]{2,1,0:T(8,128)(2,1)} async-done(((bf16[32,32,512]{2,1,0:T(8,128)(2,1)}), bf16[32,32,512]{2,1,0:T(8,128)(2,1)}, u32[]{:S(2)}, u32[]{:S(2)}) %all-to-all-start) | async-done | bytes 1048608 | tf_op jit(solution)/shard_map/all_to_all | solution.py:136
  43.8 2.1 reshape.284
  45.9 3.9 bitcast_reduce_fusion
  49.8 2.9 fusion.1
  52.8 0.1 convert_element_type.106
  52.9 0.6 copy.99
  53.5 3.8 all-to-all-start.1
  57.3 3.5 fusion.16
  60.8 2.1 copy.106
  62.9 2.6 convert_element_type.114
  65.5 7.5 %all-to-all-start.2 = ((bf16[32,32,512]{2,1,0:T(8,128)(2,1)}), bf16[32,32,512]{2,1,0:T(8,128)(2,1)}, u32[]{:S(2)}, u32[]{:S(2)}) async-start(bf16[32,32,512]{2,1,0:T(8,128)(2,1)} %convert_element_type.114), calls=%async_computation.2 | async-start | bytes 2097152 | tf_op jit(solution)/shard_map/all_to_all | solution.py:141
  73.0 0.2 all-reduce.2.cloned.1.call-start
  73.2 0.4 fusion.67
  73.6 0.1 fusion.40
  73.7 0.7 copy-done.2
  74.4 0.3 copy.114
  74.7 0.7 gather_fusion
  75.5 14.8 %all-to-all-done.2 = bf16[32,32,512]{2,1,0:T(8,128)(2,1)} async-done(((bf16[32,32,512]{2,1,0:T(8,128)(2,1)}), bf16[32,32,512]{2,1,0:T(8,128)(2,1)}, u32[]{:S(2)}, u32[]{:S(2)}) %all-to-all-start.2) | async-done | bytes 1048608 | tf_op jit(solution)/shard_map/all_to_all | solution.py:141
  90.3 2.9 bitcast_convert_fusion
  93.2 2.8 gather_fusion.1
  96.0 1.0 copy.107
  97.0 2.9 fusion.26
  99.9 1.9 convolution_convert_fusion.1
  101.9 3.2 convert_element_type.100
  105.0 43.6 %all-reduce.2.cloned.1.call-done = bf16[256,2560]{1,0:T(8,128)(2,1)} async-done(((bf16[256,2560]{1,0:T(8,128)(2,1)}), bf16[256,2560]{1,0:T(8,128)(2,1)}) %all-reduce.2.cloned.1.call-update) | async-done | bytes 1310736 | tf_op jit(solution)/shard_map/psum | solution.py:161
  148.7 1.1 fusion.34
  149.9 1.5 multiply_reduce_fusion.1
  151.4 1.4 multiply_convert_fusion.1
  152.8 1.2 stack.2
  154.0 125.6 %all_to_all.20 = bf16[32,64,2560]{2,1,0:T(8,128)(2,1)} all-to-all(bf16[32,64,2560]{2,1,0:T(8,128)(2,1)S(1)} %stack.2), channel_id=1, replica_groups=mesh['req'=32,'mlp'=4] {'req'}, dimensions={0} | all-to-all | bytes 20971520 | tf_op jit(solution)/shard_map/all_to_all | solution.py:168
  279.6 7.8 %fusion.68 = f32[2048,320]{0,1:T(8,128)} fusion(bf16[2048,2560]{1,0:T(8,128)(2,1)} %bitcast.31, bf16[2560,320]{0,1:T(8,128)(2,1)S(1)} %copy-done.8), kind=kOutput, calls=%fused_computation.110 | convolution fusion | flops 3355443200 | bytes 14745600 | tf_op jit(solution)/shard_map/dot_general | solution.py:170
  287.4 15.6 %convolution_convert_fusion = bf16[2048,2560]{1,0:T(8,128)(2,1)} fusion(bf16[320,2560]{1,0:T(8,128)(2,1)} %param.31, bf16[2048,2560]{1,0:T(8,128)(2,1)} %bitcast.31, bf16[2560,320]{0,1:T(8,128)(2,1)} %param.30, f32[2048,320]{0,1:T(8,128)} %fusion.68), kind=kOutput, calls=%fused_computation.2 | convolution fusion | flops 6722682880 | bytes 26869760 | tf_op jit(solution)/shard_map/dot_general | solution.py:174
  303.1 96.8 %reduce-scatter.2.cloned.1.call-done = bf16[64,2560]{1,0:T(8,128)(2,1)} async-done(((bf16[2048,2560]{1,0:T(8,128)(2,1)}), bf16[64,2560]{1,0:T(8,128)(2,1)}) %reduce-scatter.2.cloned.1.call-update) | async-done | bytes 327696 | tf_op jit(solution)/shard_map/reduce_scatter | solution.py:173
  399.9 1.1 fusion.35
  401.0 2.3 fusion.38
  (46 shorter events, 0.4 us)
Async XLA Ops:
  6.5 93.3 %copy-start = (bf16[512,2560]{1,0:T(8,128)(2,1)S(1)}, bf16[512,2560]{1,0:T(8,128)(2,1)}, u32[]{:S(2)}) copy-start(bf16[512,2560]{1,0:T(8,128)(2,1)} %param.26) | copy-start | bytes 7864324
  16.2 10.2 %copy-start.7 = (s32[256]{0:T(256)S(1)}, s32[256]{0:T(256)}, u32[]{:S(2)}) copy-start(s32[256]{0:T(256)} %param.35) | copy-start | bytes 3076
  16.3 10.3 %copy-start.10 = (f32[2560]{0:T(1024)S(1)}, f32[2560]{0:T(1024)}, u32[]{:S(2)}) copy-start(f32[2560]{0:T(1024)} %param.20) | copy-start | bytes 30724
  18.9 24.9 %all-to-all-start = ((bf16[32,32,512]{2,1,0:T(8,128)(2,1)}), bf16[32,32,512]{2,1,0:T(8,128)(2,1)}, u32[]{:S(2)}, u32[]{:S(2)}) async-start(bf16[32,32,512]{2,1,0:T(8,128)(2,1)} %bitcast.131), calls=%async_computation | async-start | bytes 2097152 | tf_op jit(solution)/shard_map/all_to_all | solution.py:136
  26.6 19.3 %copy-start.3 = (bf16[1,512,256]{2,1,0:T(8,128)(2,1)S(1)}, bf16[1,512,256]{2,1,0:T(8,128)(2,1)}, u32[]{:S(2)}) copy-start(bf16[1,512,256]{2,1,0:T(8,128)(2,1)} %param.33) | copy-start | bytes 786436
  49.8 7.4 %copy-start.9 = (bf16[1,512,256]{2,1,0:T(8,128)(2,1)S(1)}, bf16[1,512,256]{2,1,0:T(8,128)(2,1)}, u32[]{:S(2)}) copy-start(bf16[1,512,256]{2,1,0:T(8,128)(2,1)} %param.34) | copy-start | bytes 786436
  53.5 12.0 %all-to-all-start.1 = ((bf16[32,32,2]{1,2,0:T(2,128)(2,1)}), bf16[32,32,2]{1,2,0:T(2,128)(2,1)S(1)}, u32[]{:S(2)}, u32[]{:S(2)}) async-start(bf16[32,32,2]{1,2,0:T(2,128)(2,1)} %copy.99), calls=%async_computation.1 | async-start | bytes 32768 | tf_op jit(solution)/shard_map/all_to_all | solution.py:144
  62.9 10.3 %copy-start.12 = (f32[256]{0:T(256)S(1)}, f32[256]{0:T(256)}, u32[]{:S(2)}) copy-start(f32[256]{0:T(256)} %param.25) | copy-start | bytes 3076
  62.9 10.3 %copy-start.13 = (f32[256,256]{0,1:T(8,128)S(1)}, f32[256,256]{0,1:T(8,128)}, u32[]{:S(2)}) copy-start(f32[256,256]{0,1:T(8,128)} %get-tuple-element.12) | copy-start | bytes 786436
  65.5 24.8 %all-to-all-start.2 = ((bf16[32,32,512]{2,1,0:T(8,128)(2,1)}), bf16[32,32,512]{2,1,0:T(8,128)(2,1)}, u32[]{:S(2)}, u32[]{:S(2)}) async-start(bf16[32,32,512]{2,1,0:T(8,128)(2,1)} %convert_element_type.114), calls=%async_computation.2 | async-start | bytes 2097152 | tf_op jit(solution)/shard_map/all_to_all | solution.py:141
  73.0 75.7 %all-reduce.2.cloned.1.call-start = ((), (), s32[]{:S(2)}) async-start(), calls=%async_computation.5 | async-start | bytes 2621440 | tf_op jit(solution)/shard_map/psum | solution.py:161
  73.6 0.8 copy-start.2
  93.1 3.8 copy-start.11
  101.8 48.0 %copy-start.4 = (f32[2560]{0:T(1024)S(1)}, f32[2560]{0:T(1024)}, u32[]{:S(2)}) copy-start(f32[2560]{0:T(1024)} %param.27) | copy-start | bytes 30724
  101.8 298.1 %reduce-scatter.2.cloned.1.call-start = ((), (), s32[]{:S(2)}) async-start(), calls=%async_computation.6 | async-start | bytes 10813440 | tf_op jit(solution)/shard_map/reduce_scatter | solution.py:173
  101.9 49.5 %copy-start.5 = (f32[2560]{0:T(1024)S(1)}, f32[2560]{0:T(1024)}, u32[]{:S(2)}) copy-start(f32[2560]{0:T(1024)} %param.28) | copy-start | bytes 30724
  154.0 125.6 %copy-start.8 = (bf16[2560,320]{0,1:T(8,128)(2,1)S(1)}, bf16[2560,320]{0,1:T(8,128)(2,1)}, u32[]{:S(2)}) copy-start(bf16[2560,320]{0,1:T(8,128)(2,1)} %param.29) | copy-start | bytes 4915204
  303.0 98.0 %copy-start.6 = (f32[2560]{0:T(1024)S(1)}, f32[2560]{0:T(1024)}, u32[]{:S(2)}) copy-start(f32[2560]{0:T(1024)} %param.32) | copy-start | bytes 30724
  303.0 100.3 %copy-start.1 = (bf16[512,2560]{1,0:T(8,128)(2,1)S(1)}, bf16[512,2560]{1,0:T(8,128)(2,1)}, u32[]{:S(2)}) copy-start(bf16[512,2560]{1,0:T(8,128)(2,1)} %param.26) | copy-start | bytes 7864324
Sparse Core Ops, SparseCore 0:
  101.9 46.6 all-reduce.1
  303.2 96.6 reduce-scatter.1
